TPU v7x, 256 devices: a whole 4x4x8 slice. The times are simulated.
256 devices in a mesh: leaf: 16 (over x, y), blk: 16 (over z, core).
Axes of the slice: x: 4, y: 4, z: 8, core: 2. Of those that a mesh axis runs over, the one named last changes fastest.
Arguments:
- near_tiles: bfloat16 [128, 16, 512, 512], P('leaf', 'blk'), may hold values from -0.25 to 0.25
- near_cols: int32 [128, 16], P('leaf', 'blk'), may hold values from 0 to 127, as said below
- near_count: int32 [128], P('leaf'), may hold values from 1 to 16, as said below
- probes: bfloat16 [128, 512, 512], P('leaf'), may hold values from -6 to 6
- mixing: float32 [512, 64], replicated, may hold values from -0.25 to 0.25
- far_tiles: bfloat16 [128, 16, 512, 512], P('leaf', 'blk'), may hold values from -6 to 6
- far_cols: int32 [128, 16], P('leaf', 'blk'), may hold values from 0 to 127, as said below
Outputs:
- coupling: float32 [128, 16, 64, 64], P('leaf', 'blk')
- root_part: float32 [128, 64, 64], P('leaf')
Inputs may be any that keep to these rules, and one draw needn't show every extreme that they name: near_cols[r, k] lies within 8 of r; the slots below near_count[r] name distinct clusters. Slots at or past near_count[r] hold arbitrary tiles that must be ignored. far_cols[r, j] differs from r by more than 8.
All inputs are finite; a program needn't handle non-finite values.
Results may differ from a plain program's by a relative error of at most 0.0041.
Values may be sent and summed in bfloat16 or wider, within the bound.
No kernel may reach another device: no remote copies, remote signals or barrier semaphores. Data moves between devices by JAX's collectives and lax.ppermute only.
A program may use at most 128 MiB of HBM per device.

v0:
```python
import math
import jax
import jax.numpy as jnp
from jax import lax
from jax.sharding import PartitionSpec as P

RANK = 64
REACH = 8
highest = lax.Precision.HIGHEST


def padded(value, sides, width):
    for axis, dim in sides:
        peers, length = (lax.axis_size(axis), value.shape[dim])
        up = [(i, (i + 1) % peers) for i in range(peers - 1)]
        down = [(j, i) for i, j in up]
        last = lax.slice_in_dim(value, length - width, length, axis=dim)
        leading = lax.slice_in_dim(value, 0, width, axis=dim)
        before = lax.ppermute(last, axis, up)
        after = lax.ppermute(leading, axis, down)
        value = jnp.concatenate([before, value, after], axis=dim)
    return value


def partner_2(block, axis, apart):
    count = lax.axis_size(axis)
    route = []
    for low in range(count):
        high = low | 1 << apart
        if high != low and high < count:
            route += [(low, high), (high, low)]
    return lax.ppermute(block, axis, route)


def basis_from(gram_matrix, mixed_rows):
    lower_factor = jnp.linalg.cholesky(gram_matrix)
    solved = jax.scipy.linalg.solve_triangular(
        lower_factor, jnp.swapaxes(mixed_rows, -1, -2), lower=True
    )
    return jnp.swapaxes(solved, -1, -2)


def merge(stacked, mixing):
    mixed_rows = jnp.einsum("...mp,pk->...mk", stacked, mixing, precision=highest)
    gram_matrix = jnp.einsum("...mk,...ml->...kl", mixed_rows, mixed_rows, precision=highest)
    transfer = basis_from(gram_matrix, mixed_rows)
    merged = jnp.einsum("...mk,...mp->...kp", transfer, stacked, precision=highest)
    return (transfer, merged)


def shards(near_tiles, near_cols, near_count, probes, mixing, far_tiles, far_cols):
    local_rows = probes.shape[0]
    near_dev = near_tiles.shape[1]
    leaf_pos = lax.axis_index("leaf")
    blk_pos = lax.axis_index("blk")
    subtrees = lax.axis_size("leaf")
    clusters = local_rows * subtrees
    first_cluster = leaf_pos * local_rows - REACH
    window = padded(probes, (("leaf", 0),), REACH)

    def leaf_sketch(row_index):
        running = jnp.zeros((probes.shape[1], probes.shape[2]), jnp.float32)
        column = near_cols[row_index, 0] - first_cluster
        probe_block = lax.dynamic_index_in_dim(window, column, 0, keepdims=False)
        near_tile = near_tiles[row_index, 0]
        is_live = blk_pos * near_dev + 0 < near_count[row_index]
        running = lax.cond(
            is_live,
            lambda current: jnp.dot(near_tile, probe_block, preferred_element_type=jnp.float32),
            lambda current: current,
            running,
        )
        return running

    partial_sketch = lax.map(leaf_sketch, jnp.arange(local_rows))
    sketch_rows = lax.psum_scatter(partial_sketch, "blk", scatter_dimension=1, tiled=True)
    mixed_rows = jnp.einsum("rbp,pk->rbk", sketch_rows, mixing, precision=highest)
    gram_part = jnp.einsum("rbk,rbl->rkl", mixed_rows, mixed_rows, precision=highest)
    gram_matrix = lax.psum(gram_part, "blk")
    basis_part = basis_from(gram_matrix, mixed_rows)
    proj_part = jnp.einsum("rbk,rbp->rkp", basis_part, sketch_rows, precision=highest)
    leaf_proj = lax.psum(proj_part, "blk")
    basis_low = lax.all_gather(basis_part.astype(jnp.bfloat16), "blk", axis=1, tiled=True)
    all_bases = lax.all_gather(basis_low, "leaf", axis=0, tiled=True)
    far_basis = all_bases[far_cols]
    far_image = jnp.einsum(
        "rjab,rjbk->rjak", far_tiles, far_basis, preferred_element_type=jnp.float32
    )
    coupling = jnp.einsum(
        "rak,rjal->rjkl", basis_low.astype(jnp.float32), far_image, precision=highest
    )
    sub_stack = leaf_proj.reshape(local_rows * RANK, leaf_proj.shape[2])
    sub_transfer, node_sketch = merge(sub_stack, mixing)
    levels = subtrees.bit_length() - 1
    path_factor = jnp.eye(RANK, dtype=jnp.float32)
    for depth_index in range(levels):
        partner = partner_2(node_sketch.astype(jnp.bfloat16), "leaf", depth_index).astype(
            node_sketch.dtype
        )
        is_upper = leaf_pos >> depth_index & 1
        lower_half = jnp.where(is_upper == 1, partner, node_sketch)
        upper_half = jnp.where(is_upper == 1, node_sketch, partner)
        transfer, node_sketch = merge(jnp.concatenate([lower_half, upper_half], 0), mixing)
        picked = lax.dynamic_slice_in_dim(transfer, is_upper * RANK, RANK, 0)
        path_factor = jnp.dot(path_factor, picked, precision=highest)
    sub_blocks = sub_transfer.reshape(local_rows, RANK, RANK)
    root_part = jnp.einsum("cab,bd->cad", sub_blocks, path_factor, precision=highest)
    root_part = root_part * math.sqrt(clusters * RANK)
    return (coupling, root_part)


def solution(mesh):
    in_specs = (
        P("leaf", "blk", None, None),
        P("leaf", "blk"),
        P("leaf"),
        P("leaf", None, None),
        P(),
        P("leaf", "blk", None, None),
        P("leaf", "blk"),
    )
    out_specs = (P("leaf", "blk", None, None), P("leaf", None, None))
    return jax.shard_map(shards, mesh=mesh, in_specs=in_specs, out_specs=out_specs, check_vma=False)
```

profile of v0, /device:TPU:22, one launch (start us, length us, event | category | flops | bytes accessed | tf_op | source)
XLA Modules:
  0.0 679.8 jit_solution(7134080984132930772)
XLA Ops:
  13.1 88.6 %collective-permute-done = bf16[8,512,512]{2,1,0:T(8,128)(2,1)} collective-permute-done((bf16[8,512,512]{2,1,0:T(8,128)(2,1)}, bf16[8,512,512]{2,1,0:T(8,128)(2,1)}, u32[]{:S(2)}, u32[]{:S(2)}) %collective-permute-start) | collective-permute-done | bytes 4194336 | tf_op jit(solution)/shard_map/ppermute | solution.py:19
  104.7 10.8 %pad_maximum_fusion = bf16[24,512,512]{2,1,0:T(8,128)(2,1)} fusion(bf16[8,512,512]{2,1,0:T(8,128)(2,1)} %collective-permute-done.1, bf16[8,512,512]{2,1,0:T(8,128)(2,1)} %param.17, bf16[8,512,512]{2,1,0:T(8,128)(2,1)} %collective-permute-done), kind=kLoop, calls=%fused_computation.9 | loop fusion | flops 12582912 | bytes 25165824 | tf_op jit(solution)/shard_map/concatenate | solution.py:21
  115.4 60.4 %while.10 = (s32[]{:T(128)}, f32[8,512,512]{2,1,0:T(8,128)}, s32[8]{0:T(128)S(1)}, s32[8]{0:T(128)S(1)}, s32[]{:T(128)}, /*index=5*/bf16[8,1,512,512]{3,2,1,0:T(...) while((s32[]{:T(128)}, f32[8,512,512]{2,1,0:T(8,128)}, ...), condition=%wide.region_3.4_spmd, body=%wide.region_0.3_spmd.sunk | while | flops 268435456 | bytes 4195627 | solution.py:75
  175.9 75.0 %reduce-scatter.2.cloned.1.call-done = f32[8,32,512]{2,1,0:T(8,128)} async-done(((f32[8,512,512]{2,1,0:T(8,128)}), f32[8,32,512]{2,1,0:T(8,128)}) %reduce-scatter.2.cloned.1.call-update) | async-done | bytes 524304 | tf_op jit(solution)/shard_map/reduce_scatter | solution.py:76
  253.9 108.8 %all-reduce.3.cloned.1.call-done = f32[8,64,64]{1,2,0:T(8,128)} async-done(((f32[8,64,64]{1,2,0:T(8,128)}), f32[8,64,64]{1,2,0:T(8,128)}) %all-reduce.3.cloned.1.call-update) | async-done | bytes 131088 | tf_op jit(solution)/shard_map/psum | solution.py:79
  364.8 46.9 %custom-call.17 = f32[8,64,64]{2,1,0:T(8,128)S(1)} custom-call(f32[8,64,64]{2,1,0:T(8,128)S(1)} %fusion.13), custom_call_target="Cholesky" | custom-call | tf_op jit(solution)/shard_map/jit(cholesky)/cholesky | solution.py:36
  411.9 39.3 %custom-call.18 = f32[8,1,64,64]{2,3,1,0:T(8,128)S(1)} custom-call(f32[8,1,64,64]{3,2,1,0:T(8,128)S(1)} %select_bitcast_fusion), custom_call_target="InvertDiagBlocksLowerTriangular" | custom-call | tf_op jit(solution)/shard_map/jit(_solve_triangular)/vmap()/triangular_solve | solution.py:37
  454.9 18.4 %all_gather.6 = bf16[8,512,64]{2,1,0:T(8,128)(2,1)S(1)} all-gather(bf16[8,32,64]{2,1,0:T(8,128)(2,1)S(1)} %convert_bitcast_fusion), channel_id=1, replica_groups=mesh['leaf'=16,'blk'=16] {'blk'}, dimensions={1}, use_global_device_ids=true | all-gather | bytes 557056 | tf_op jit(solution)/shard_map/all_gather | solution.py:83
  474.5 93.2 %all-reduce.5.cloned.1.call-done = f32[512,512]{1,0:T(8,128)} async-done(((f32[512,512]{1,0:T(8,128)}), f32[512,512]{1,0:T(8,128)}) %all-reduce.5.cloned.1.call-update) | async-done | bytes 1048592 | tf_op jit(solution)/shard_map/psum | solution.py:82
  570.5 5.8 cholesky.127
  577.7 4.9 custom-call.19
  586.5 4.7 collective-permute-done.2
  591.9 5.8 cholesky.138
  599.1 4.9 custom-call.23
  605.3 5.9 collective-permute-done.3
  611.9 5.8 cholesky.149
  619.1 4.9 custom-call.24
  625.4 5.0 collective-permute-done.4
  631.1 5.8 cholesky.160
  638.3 4.9 custom-call.25
  645.6 4.3 collective-permute-done.5
  650.5 5.8 cholesky.171
  657.7 4.9 custom-call.26
  664.2 4.0 gather_fusion
  (146 shorter events, 105.0 us)
Async XLA Ops:
  7.2 243.7 %copy-start = (f32[512,64]{0,1:T(8,128)S(1)}, f32[512,64]{0,1:T(8,128)}, u32[]{:S(2)}) copy-start(f32[512,64]{0,1:T(8,128)} %param.18) | copy-start | bytes 393220
  7.2 243.7 %reduce-scatter.2.cloned.1.call-start = ((), (), s32[]{:S(2)}) async-start(), calls=%async_computation.1 | async-start | bytes 8912896 | tf_op jit(solution)/shard_map/reduce_scatter | solution.py:76
  7.2 94.5 %collective-permute-start = (bf16[8,512,512]{2,1,0:T(8,128)(2,1)}, bf16[8,512,512]{2,1,0:T(8,128)(2,1)}, u32[]{:S(2)}, u32[]{:S(2)}) collective-permute-start(bf16[8,512,512]{2,1,0:T(8,128)(2,1)} %param.17), channel_id=1, source_target_pairs={{0,16},{16,32},{32,48},{48,64},{64,80},{80,96},{96,112},{112,128},... | collective-permute-start | bytes 12582920 | tf_op jit(solution)/shard_map/ppermute | solution.py:19
  10.4 94.2 %collective-permute-start.1 = (bf16[8,512,512]{2,1,0:T(8,128)(2,1)}, bf16[8,512,512]{2,1,0:T(8,128)(2,1)}, u32[]{:S(2)}, u32[]{:S(2)}) collective-permute-start(bf16[8,512,512]{2,1,0:T(8,128)(2,1)} %param.17), channel_id=1, source_target_pairs={{16,0},{32,16},{48,32},{64,48},{80,64},{96,80},{112,96},{128,112},... | collective-permute-start | bytes 12582920 | tf_op jit(solution)/shard_map/ppermute | solution.py:20
  13.1 102.3 %copy-start.1 = (s32[8]{0:T(128)S(1)}, s32[8]{0:T(128)}, u32[]{:S(2)}) copy-start(s32[8]{0:T(128)} %param.16) | copy-start | bytes 100
  13.1 102.3 %copy-start.2 = (s32[8,1]{0,1:T(1,128)S(1)}, s32[8,1]{0,1:T(1,128)}, u32[]{:S(2)}) copy-start(s32[8,1]{0,1:T(1,128)} %param.15) | copy-start | bytes 100
  175.8 298.7 %copy-start.3 = (s32[8,1]{0,1:T(1,128)S(1)}, s32[8,1]{0,1:T(1,128)}, u32[]{:S(2)}) copy-start(s32[8,1]{0,1:T(1,128)} %param.20) | copy-start | bytes 100
  175.8 186.9 %all-reduce.3.cloned.1.call-start = ((), (), s32[]{:S(2)}) async-start(), calls=%async_computation.2 | async-start | bytes 524288 | tf_op jit(solution)/shard_map/psum | solution.py:79
  253.8 314.0 %all-reduce.5.cloned.1.call-start = ((), (), s32[]{:S(2)}) async-start(), calls=%async_computation.4 | async-start | bytes 2097152 | tf_op jit(solution)/shard_map/psum | solution.py:82
  454.8 209.4 %all-gather.2.cloned.1.call-start = ((), (), s32[]{:S(2)}) async-start(), calls=%async_computation.3 | async-start | bytes 8912896 | tf_op jit(solution)/shard_map/all_gather | solution.py:84
  584.9 6.3 collective-permute-start.2
  604.5 6.7 collective-permute-start.3
  624.5 5.9 collective-permute-start.4
  643.7 6.1 collective-permute-start.5
Sparse Core Ops, SparseCore 0:
  175.9 74.8 reduce-scatter.1
  253.9 108.7 all-reduce.2
  454.9 112.7 all-reduce.4
  570.0 76.4 all-gather.1
where the time goes:
time: 681 us; the launch traced here: 680 us
  waiting for transfers between devices  388 us (57%)
  other arithmetic  159 us (23%)
  matrix products  35 us (5%)
  local copies, waits for them, and re-layouts  30.2 us (4%)
  loops' own time  24.6 us (4%)
  blocking collectives  18.4 us (3%)
  between operations  14.2 us (2%)
  starting transfers between devices  10.2 us (1%)
    psum x1, waiting for transfers between devices, shards(): gram_matrix = lax.psum(gram_part, 'blk')  109 us
    psum x1, waiting for transfers between devices, shards(): leaf_proj = lax.psum(proj_part, 'blk')  93.2 us
    ppermute x1, waiting for transfers between devices, padded(): before = lax.ppermute(last, axis, up)  88.6 us
    another operation x19, other arithmetic, basis_from(): lower_factor = jnp.linalg.cholesky(gram_matrix)  79.7 us
    reduce_scatter x1, waiting for transfers between devices, shards(): lax.psum_scatter(partial_sketch, 'blk', scatter_dimension=1, tiled=True)  75 us
    another operation x13, other arithmetic, basis_from(): jax.scipy.linalg.solve_triangular(lower_factor, jnp.swapaxes(mixed_rows,...  67.2 us
    another operation x1, loops' own time, shards(): partial_sketch = lax.map(leaf_sketch, jnp.arange(local_rows))  19.8 us
    ppermute x4, waiting for transfers between devices, partner_2(): return lax.ppermute(block, axis, route)  19.7 us
  transfers between devices with their start and end apart: 10, of which 9 were waited for; matrix products, arithmetic and copies ran while one was open for 11% of the time, Pallas kernels for 0%

commit v1 on v0

--- a/solution.py
+++ b/solution.py
@@ -7,6 +7,14 @@
 RANK = 64
 REACH = 8
 highest = lax.Precision.HIGHEST
+
+
+def add_in_pairs(x, mesh_axis):
+    count, total = (lax.axis_size(mesh_axis), x)
+    for hop in [1 << k for k in range(count.bit_length() - 1)]:
+        swap = [(i, i ^ hop) for i in range(count)]
+        total = total + lax.ppermute(total, mesh_axis, swap)
+    return total
 
 
 def padded(value, sides, width):
@@ -79,7 +87,7 @@
     gram_matrix = lax.psum(gram_part, "blk")
     basis_part = basis_from(gram_matrix, mixed_rows)
     proj_part = jnp.einsum("rbk,rbp->rkp", basis_part, sketch_rows, precision=highest)
-    leaf_proj = lax.psum(proj_part, "blk")
+    leaf_proj = add_in_pairs(proj_part, "blk")
     basis_low = lax.all_gather(basis_part.astype(jnp.bfloat16), "blk", axis=1, tiled=True)
     all_bases = lax.all_gather(basis_low, "leaf", axis=0, tiled=True)
     far_basis = all_bases[far_cols]

time: 681 us -> 710 us (1.043)
  waiting for transfers between devices: 388 us -> 410 us
  starting transfers between devices: 10.2 us -> 18.8 us
    ppermute x0 -> x4, waiting for transfers between devices: none -> 120 us  [add_in_pairs(): total = total + lax.ppermute(total, mesh_axis, swap)]
    psum x1 -> x0, waiting for transfers between devices: 93.2 us -> none  [shards(): leaf_proj = lax.psum(proj_part, 'blk')]
    ppermute x0 -> x4, starting transfers between devices: none -> 8.18 us  [add_in_pairs(): total = total + lax.ppermute(total, mesh_axis, swap)]
  transfers between devices with their start and end apart: 10 -> 13, of which waited for: 9 -> 12; matrix products, arithmetic and copies ran while one was open for 11% -> 10% of each run, Pallas kernels for 0% -> 0%
where the time goes in v1:
time: 710 us; the launch traced here: 709 us
  waiting for transfers between devices  410 us (58%)
  other arithmetic  161 us (23%)
  matrix products  31.4 us (4%)
  local copies, waits for them, and re-layouts  30.2 us (4%)
  loops' own time  24.6 us (3%)
  starting transfers between devices  18.8 us (3%)
  blocking collectives  18.4 us (3%)
  between operations  14.2 us (2%)
    ppermute x4, waiting for transfers between devices, add_in_pairs(): total = total + lax.ppermute(total, mesh_axis, swap)  120 us
    psum x1, waiting for transfers between devices, shards(): gram_matrix = lax.psum(gram_part, 'blk')  109 us
    ppermute x1, waiting for transfers between devices, padded(): before = lax.ppermute(last, axis, up)  88.6 us
    another operation x19, other arithmetic, basis_from(): lower_factor = jnp.linalg.cholesky(gram_matrix)  79.7 us
    reduce_scatter x1, waiting for transfers between devices, shards(): lax.psum_scatter(partial_sketch, 'blk', scatter_dimension=1, tiled=True)  75 us
    another operation x13, other arithmetic, basis_from(): jax.scipy.linalg.solve_triangular(lower_factor, jnp.swapaxes(mixed_rows,...  67.2 us
    another operation x1, loops' own time, shards(): partial_sketch = lax.map(leaf_sketch, jnp.arange(local_rows))  19.8 us
    all_gather x1, blocking collectives, shards(): lax.all_gather(basis_part.astype(jnp.bfloat16), 'blk', axis=1, tiled=True)  18.4 us
  transfers between devices with their start and end apart: 13, of which 12 were waited for; matrix products, arithmetic and copies ran while one was open for 10% of the time, Pallas kernels for 0%

profile of v1, /device:TPU:22, one launch (start us, length us, event | category | flops | bytes accessed | tf_op | source)
XLA Modules:
  0.0 708.6 jit_solution(5096418935061471566)
XLA Ops:
  13.1 88.6 %collective-permute-done = bf16[8,512,512]{2,1,0:T(8,128)(2,1)} collective-permute-done((bf16[8,512,512]{2,1,0:T(8,128)(2,1)}, bf16[8,512,512]{2,1,0:T(8,128)(2,1)}, u32[]{:S(2)}, u32[]{:S(2)}) %collective-permute-start) | collective-permute-done | bytes 4194336 | tf_op jit(solution)/shard_map/ppermute | solution.py:27
  104.7 10.8 %pad_maximum_fusion = bf16[24,512,512]{2,1,0:T(8,128)(2,1)} fusion(bf16[8,512,512]{2,1,0:T(8,128)(2,1)} %collective-permute-done.1, bf16[8,512,512]{2,1,0:T(8,128)(2,1)} %param.17, bf16[8,512,512]{2,1,0:T(8,128)(2,1)} %collective-permute-done), kind=kLoop, calls=%fused_computation.9 | loop fusion | flops 12582912 | bytes 25165824 | tf_op jit(solution)/shard_map/concatenate | solution.py:29
  115.4 60.4 %while.10 = (s32[]{:T(128)}, f32[8,512,512]{2,1,0:T(8,128)}, s32[8]{0:T(128)S(1)}, s32[8]{0:T(128)S(1)}, s32[]{:T(128)}, /*index=5*/bf16[8,1,512,512]{3,2,1,0:T(...) while((s32[]{:T(128)}, f32[8,512,512]{2,1,0:T(8,128)}, ...), condition=%wide.region_3.4_spmd, body=%wide.region_0.3_spmd.sunk | while | flops 268435456 | bytes 4195627 | solution.py:83
  175.9 75.0 %reduce-scatter.2.cloned.1.call-done = f32[8,32,512]{2,1,0:T(8,128)} async-done(((f32[8,512,512]{2,1,0:T(8,128)}), f32[8,32,512]{2,1,0:T(8,128)}) %reduce-scatter.2.cloned.1.call-update) | async-done | bytes 524304 | tf_op jit(solution)/shard_map/reduce_scatter | solution.py:84
  253.9 108.8 %all-reduce.2.cloned.1.call-done = f32[8,64,64]{1,2,0:T(8,128)} async-done(((f32[8,64,64]{1,2,0:T(8,128)}), f32[8,64,64]{1,2,0:T(8,128)}) %all-reduce.2.cloned.1.call-update) | async-done | bytes 131088 | tf_op jit(solution)/shard_map/psum | solution.py:87
  364.8 46.9 %custom-call.17 = f32[8,64,64]{2,1,0:T(8,128)S(1)} custom-call(f32[8,64,64]{2,1,0:T(8,128)S(1)} %fusion.13), custom_call_target="Cholesky" | custom-call | tf_op jit(solution)/shard_map/jit(cholesky)/cholesky | solution.py:44
  412.0 39.3 %custom-call.18 = f32[8,1,64,64]{2,3,1,0:T(8,128)S(1)} custom-call(f32[8,1,64,64]{3,2,1,0:T(8,128)S(1)} %select_bitcast_fusion), custom_call_target="InvertDiagBlocksLowerTriangular" | custom-call | tf_op jit(solution)/shard_map/jit(_solve_triangular)/vmap()/triangular_solve | solution.py:45
  451.7 18.4 %all_gather.6 = bf16[8,512,64]{2,1,0:T(8,128)(2,1)S(1)} all-gather(bf16[8,32,64]{2,1,0:T(8,128)(2,1)S(1)} %convert_bitcast_fusion), channel_id=1, replica_groups=mesh['leaf'=16,'blk'=16] {'blk'}, dimensions={1}, use_global_device_ids=true | all-gather | bytes 557056 | tf_op jit(solution)/shard_map/all_gather | solution.py:91
  477.1 24.6 %collective-permute-done.3 = f32[8,64,512]{2,1,0:T(8,128)S(1)} collective-permute-done((f32[8,64,512]{2,1,0:T(8,128)S(1)}, f32[8,64,512]{2,1,0:T(8,128)S(1)}, u32[]{:S(2)}, u32[]{:S(2)}) %collective-permute-start.3) | collective-permute-done | bytes 1048608 | tf_op jit(solution)/shard_map/ppermute | solution.py:16
  503.8 46.1 %collective-permute-done.4 = f32[8,64,512]{2,1,0:T(8,128)S(1)} collective-permute-done((f32[8,64,512]{2,1,0:T(8,128)S(1)}, f32[8,64,512]{2,1,0:T(8,128)S(1)}, u32[]{:S(2)}, u32[]{:S(2)}) %collective-permute-start.4) | collective-permute-done | bytes 1048608 | tf_op jit(solution)/shard_map/ppermute | solution.py:16
  550.1 4.9 collective-permute-start.5
  555.1 46.8 %collective-permute-done.5 = f32[8,64,512]{2,1,0:T(8,128)} collective-permute-done((f32[8,64,512]{2,1,0:T(8,128)S(1)}, f32[8,64,512]{2,1,0:T(8,128)}, u32[]{:S(2)}, u32[]{:S(2)}) %collective-permute-start.5) | collective-permute-done | bytes 1048608 | tf_op jit(solution)/shard_map/ppermute | solution.py:16
  604.9 5.8 cholesky.127
  612.0 4.9 custom-call.19
  623.1 5.8 cholesky.138
  630.3 4.9 custom-call.23
  636.6 5.0 collective-permute-done.7
  642.3 5.8 cholesky.149
  649.5 4.9 custom-call.24
  660.2 5.8 cholesky.160
  667.4 4.9 custom-call.25
  674.6 4.0 collective-permute-done.9
  679.4 5.8 cholesky.171
  686.6 4.9 custom-call.26
  (155 shorter events, 119.3 us)
Async XLA Ops:
  7.2 243.7 %copy-start = (f32[512,64]{0,1:T(8,128)S(1)}, f32[512,64]{0,1:T(8,128)}, u32[]{:S(2)}) copy-start(f32[512,64]{0,1:T(8,128)} %param.18) | copy-start | bytes 393220
  7.2 243.7 %reduce-scatter.2.cloned.1.call-start = ((), (), s32[]{:S(2)}) async-start(), calls=%async_computation.1 | async-start | bytes 8912896 | tf_op jit(solution)/shard_map/reduce_scatter | solution.py:84
  7.2 94.5 %collective-permute-start = (bf16[8,512,512]{2,1,0:T(8,128)(2,1)}, bf16[8,512,512]{2,1,0:T(8,128)(2,1)}, u32[]{:S(2)}, u32[]{:S(2)}) collective-permute-start(bf16[8,512,512]{2,1,0:T(8,128)(2,1)} %param.17), channel_id=1, source_target_pairs={{0,16},{16,32},{32,48},{48,64},{64,80},{80,96},{96,112},{112,128},... | collective-permute-start | bytes 12582920 | tf_op jit(solution)/shard_map/ppermute | solution.py:27
  10.4 94.2 %collective-permute-start.1 = (bf16[8,512,512]{2,1,0:T(8,128)(2,1)}, bf16[8,512,512]{2,1,0:T(8,128)(2,1)}, u32[]{:S(2)}, u32[]{:S(2)}) collective-permute-start(bf16[8,512,512]{2,1,0:T(8,128)(2,1)} %param.17), channel_id=1, source_target_pairs={{16,0},{32,16},{48,32},{64,48},{80,64},{96,80},{112,96},{128,112},... | collective-permute-start | bytes 12582920 | tf_op jit(solution)/shard_map/ppermute | solution.py:28
  13.1 102.3 %copy-start.1 = (s32[8]{0:T(128)S(1)}, s32[8]{0:T(128)}, u32[]{:S(2)}) copy-start(s32[8]{0:T(128)} %param.16) | copy-start | bytes 100
  13.1 102.3 %copy-start.2 = (s32[8,1]{0,1:T(1,128)S(1)}, s32[8,1]{0,1:T(1,128)}, u32[]{:S(2)}) copy-start(s32[8,1]{0,1:T(1,128)} %param.15) | copy-start | bytes 100
  175.8 186.9 %all-reduce.2.cloned.1.call-start = ((), (), s32[]{:S(2)}) async-start(), calls=%async_computation.2 | async-start | bytes 524288 | tf_op jit(solution)/shard_map/psum | solution.py:87
  253.8 439.3 %all-gather.2.cloned.1.call-start = ((), (), s32[]{:S(2)}) async-start(), calls=%async_computation.3 | async-start | bytes 8912896 | tf_op jit(solution)/shard_map/all_gather | solution.py:92
  363.8 191.3 %copy-start.3 = (s32[8,1]{0,1:T(1,128)S(1)}, s32[8,1]{0,1:T(1,128)}, u32[]{:S(2)}) copy-start(s32[8,1]{0,1:T(1,128)} %param.20) | copy-start | bytes 100
  473.3 2.7 collective-permute-start.2
  476.2 25.5 %collective-permute-start.3 = (f32[8,64,512]{2,1,0:T(8,128)S(1)}, f32[8,64,512]{2,1,0:T(8,128)S(1)}, u32[]{:S(2)}, u32[]{:S(2)}) collective-permute-start(f32[8,64,512]{2,1,0:T(8,128)S(1)} %add.73), channel_id=1, source_target_pairs={{0,2},{1,3},{2,0},{3,1},{4,6},{5,7},{6,4},{7,5},{8,10},{9,11},{10,... | collective-permute-start | bytes 3145736 | tf_op jit(solution)/shard_map/ppermute | solution.py:16
  501.9 48.0 %collective-permute-start.4 = (f32[8,64,512]{2,1,0:T(8,128)S(1)}, f32[8,64,512]{2,1,0:T(8,128)S(1)}, u32[]{:S(2)}, u32[]{:S(2)}) collective-permute-start(f32[8,64,512]{2,1,0:T(8,128)S(1)} %add.74), channel_id=1, source_target_pairs={{0,4},{1,5},{2,6},{3,7},{4,0},{5,1},{6,2},{7,3},{8,12},{9,13},{10,... | collective-permute-start | bytes 3145736 | tf_op jit(solution)/shard_map/ppermute | solution.py:16
  550.1 51.8 %collective-permute-start.5 = (f32[8,64,512]{2,1,0:T(8,128)S(1)}, f32[8,64,512]{2,1,0:T(8,128)}, u32[]{:S(2)}, u32[]{:S(2)}) collective-permute-start(f32[8,64,512]{2,1,0:T(8,128)S(1)} %add.75), channel_id=1, source_target_pairs={{0,8},{1,9},{2,10},{3,11},{4,12},{5,13},{6,14},{7,15},{8,0},{9,1},... | collective-permute-start | bytes 3145736 | tf_op jit(solution)/shard_map/ppermute | solution.py:16
  618.0 4.3 collective-permute-start.6
  635.7 5.9 collective-permute-start.7
  654.9 4.6 collective-permute-start.8
  672.8 5.9 collective-permute-start.9
Sparse Core Ops, SparseCore 0:
  175.9 74.8 reduce-scatter.1
  253.9 108.7 all-reduce.1
  471.3 74.4 all-gather.1
